TPU v7x, 32 devices: a whole 2x2x4 slice. The times are simulated.
32 devices in a mesh: dp: 2 (over y), gx: 4 (over z), gy: 4 (over x, core).
Axes of the slice: x: 2, y: 2, z: 4, core: 2. Of those that a mesh axis runs over, the one named last changes fastest.
Arguments:
- block_input: bfloat16 [3, 2, 2048, 1280], P(None, 'dp', ('gx', 'gy')), may hold values from -6 to 6
- picture: int32 [3, 2, 2048], P(None, 'dp'), may hold values from 0 to 24, as said below
- position: int32 [2, 3, 2, 2048], P(None, None, 'dp'), may hold values from 0 to 31, as said below
- patch_mask: int32 [3, 2, 2048], P(None, 'dp'), may hold values from 0 to 1, as said below
- gain_attn: float32 [1280], replicated, may hold values from 0.5 to 1.5
- shift_attn: float32 [1280], replicated, may hold values from -3 to 3
- w_query: bfloat16 [1280, 1280], P(('dp', 'gx'), 'gy'), may hold values from -0.15625 to 0.15625
- b_query: float32 [1280], replicated, may hold values from -3 to 3
- w_key: bfloat16 [1280, 1280], P(('dp', 'gx'), 'gy'), may hold values from -0.15625 to 0.15625
- b_key: float32 [1280], replicated, may hold values from -3 to 3
- w_value: bfloat16 [1280, 1280], P(('dp', 'gx'), 'gy'), may hold values from -0.15625 to 0.15625
- b_value: float32 [1280], replicated, may hold values from -3 to 3
- w_out: bfloat16 [1280, 1280], P(('dp', 'gx'), 'gy'), may hold values from -1.25 to 1.25
- b_out: float32 [1280], replicated, may hold values from -3 to 3
- gain_mlp: float32 [1280], replicated, may hold values from 0.5 to 1.5
- shift_mlp: float32 [1280], replicated, may hold values from -3 to 3
- w_up: bfloat16 [1280, 5120], P(('dp', 'gx'), 'gy'), may hold values from -0.15625 to 0.15625
- b_up: float32 [5120], replicated, may hold values from -3 to 3
- w_down: bfloat16 [1280, 5120], P(('dp', 'gx'), 'gy'), may hold values from -0.15625 to 0.15625
- b_down: float32 [1280], replicated, may hold values from -3 to 3
- out_grad: bfloat16 [3, 2, 2048, 1280], P(None, 'dp', ('gx', 'gy')), may hold values from -6 to 6
Outputs:
- block_output: bfloat16 [3, 2, 2048, 1280], P(None, 'dp', ('gx', 'gy'))
- input_grad: float32 [3, 2, 2048, 1280], P(None, 'dp', ('gx', 'gy'))
- gain_attn_grad: float32 [1280], replicated
- shift_attn_grad: float32 [1280], replicated
- w_query_grad: float32 [1280, 1280], P(('dp', 'gx'), 'gy')
- b_query_grad: float32 [1280], replicated
- w_key_grad: float32 [1280, 1280], P(('dp', 'gx'), 'gy')
- b_key_grad: float32 [1280], replicated
- w_value_grad: float32 [1280, 1280], P(('dp', 'gx'), 'gy')
- b_value_grad: float32 [1280], replicated
- w_out_grad: float32 [1280, 1280], P(('dp', 'gx'), 'gy')
- b_out_grad: float32 [1280], replicated
- gain_mlp_grad: float32 [1280], replicated
- shift_mlp_grad: float32 [1280], replicated
- w_up_grad: float32 [1280, 5120], P(('dp', 'gx'), 'gy')
- b_up_grad: float32 [5120], replicated
- w_down_grad: float32 [1280, 5120], P(('dp', 'gx'), 'gy')
- b_down_grad: float32 [1280], replicated
Inputs may be any that keep to these rules, and one draw needn't show every extreme that they name: Each row holds whole pictures one after another from slot 0, numbered 0, 1, 2, ... in that order; every picture has h by w patches, one of each row 32 by 32 and the others with sides from 10 to 31; the slots after the last picture, at least one a row, hold 24. position[0] and position[1] are the row and column of a patch within its picture, in row-major order; padding slots hold 0. `patch_mask`: 1 on the slots of pictures, 0 on the padding after them.
All inputs are finite; a program needn't handle non-finite values.
Results may differ from a plain program's by a relative error of at most 0.02.
Values may be sent and summed in bfloat16 or wider, within the bound.
No kernel may reach another device: no remote copies, remote signals or barrier semaphores. Data moves between devices by JAX's collectives and lax.ppermute only.
A program may use at most 144 MiB of HBM per device.

v0:
```python
import jax
import jax.numpy as jnp
from jax import lax
from jax.sharding import PartitionSpec as P

HEAD_DIM = 80
EPSILON = 1e-06


def layer_norm(values, norm_gain, norm_shift):
    center = values - jnp.mean(values, axis=-1, keepdims=True)
    factor = lax.rsqrt(jnp.mean(center * center, axis=-1, keepdims=True) + EPSILON)
    normal = center * factor
    return (normal * norm_gain + norm_shift, normal, factor)


def norm_back(upstream, normal, factor, norm_gain):
    shaped = upstream * norm_gain
    first_mean = jnp.mean(shaped, axis=-1, keepdims=True)
    second_mean = jnp.mean(shaped * normal, axis=-1, keepdims=True)
    return factor * (shaped - first_mean - normal * second_mean)


def rotary_tables(position_rows, first_slot, slot_total):
    quarter = HEAD_DIM // 4
    inverse = 10000.0 ** (-jnp.arange(quarter, dtype=jnp.float32) / quarter)
    picked = lax.dynamic_slice_in_dim(position_rows, first_slot, slot_total, 2).astype(jnp.float32)
    along_rows = jnp.transpose(picked[0])[:, :, None] * inverse
    along_cols = jnp.transpose(picked[1])[:, :, None] * inverse
    angles = jnp.concatenate([along_rows, along_cols, along_rows, along_cols], axis=-1)[
        :, :, None, :
    ]
    return (jnp.cos(angles), jnp.sin(angles))


def rotate(values, cos_table, sin_table):
    halfway = HEAD_DIM // 2
    turned = jnp.concatenate([-values[..., halfway:], values[..., :halfway]], axis=-1)
    return values * cos_table + turned * sin_table


def rotate_back(upstream, cos_table, sin_table):
    halfway = HEAD_DIM // 2
    moved = upstream * sin_table
    return upstream * cos_table + jnp.concatenate(
        [moved[..., halfway:], -moved[..., :halfway]], axis=-1
    )


def attention_scores(queries, keys_all, visible):
    raw = jnp.einsum(
        "qrhd,krhd->rhqk", queries, keys_all, preferred_element_type=jnp.float32
    ) * HEAD_DIM ** (-0.5)
    return jnp.where(visible[:, None], raw, -1e30)


def per_device(
    block_input,
    picture,
    position,
    patch_mask,
    gain_attn,
    shift_attn,
    w_query,
    b_query,
    w_key,
    b_key,
    w_value,
    b_value,
    w_out,
    b_out,
    gain_mlp,
    shift_mlp,
    w_up,
    b_up,
    w_down,
    b_down,
    out_grad,
):
    across = lax.axis_size("gy")
    column = lax.axis_index("gy")
    segment = lax.axis_index("gx")
    micro_count = block_input.shape[0]
    row_count = block_input.shape[1]
    own_rows = block_input.shape[2]
    slot_count = picture.shape[2]
    query_rows = own_rows * across
    head_cols = w_query.shape[1]
    hidden_cols = w_up.shape[1]
    heads_here = head_cols // HEAD_DIM
    query_start = segment * query_rows
    head_start = column * head_cols
    up_start = column * hidden_cols
    scaling = HEAD_DIM ** (-0.5)
    query_bias = lax.dynamic_slice_in_dim(b_query, head_start, head_cols)
    key_bias = lax.dynamic_slice_in_dim(b_key, head_start, head_cols)
    value_bias = lax.dynamic_slice_in_dim(b_value, head_start, head_cols)
    up_bias = lax.dynamic_slice_in_dim(b_up, up_start, hidden_cols)
    head_shape = (query_rows, row_count, heads_here, HEAD_DIM)
    grad_shards = [
        jnp.zeros(shard.shape, jnp.float32)
        for shard in (w_query, w_key, w_value, w_out, w_up, w_down)
    ]
    sum_gain_attn = jnp.zeros(gain_attn.shape, jnp.float32)
    sum_shift_attn = jnp.zeros(gain_attn.shape, jnp.float32)
    sum_query_bias = jnp.zeros((head_cols,), jnp.float32)
    sum_key_bias = jnp.zeros((head_cols,), jnp.float32)
    sum_value_bias = jnp.zeros((head_cols,), jnp.float32)
    sum_out_bias = jnp.zeros(b_out.shape, jnp.float32)
    sum_gain_mlp = jnp.zeros(gain_mlp.shape, jnp.float32)
    sum_shift_mlp = jnp.zeros(gain_mlp.shape, jnp.float32)
    sum_up_bias = jnp.zeros((hidden_cols,), jnp.float32)
    sum_down_bias = jnp.zeros(b_down.shape, jnp.float32)
    outputs = []
    input_grads = []
    for micro in range(micro_count):
        blocks = (
            lax.all_gather(w_query, ("dp", "gx"), axis=0, tiled=True),
            lax.all_gather(w_key, ("dp", "gx"), axis=0, tiled=True),
            lax.all_gather(w_value, ("dp", "gx"), axis=0, tiled=True),
            lax.all_gather(w_out, ("dp", "gx"), axis=0, tiled=True),
            lax.all_gather(w_up, ("dp", "gx"), axis=0, tiled=True),
            lax.all_gather(w_down, ("dp", "gx"), axis=0, tiled=True),
        )
        full_query, full_key, full_value, full_out, full_up, full_down = blocks
        inputs = jnp.transpose(block_input[micro], (1, 0, 2)).astype(jnp.float32)
        normed, normal_one, factor_one = layer_norm(inputs, gain_attn, shift_attn)
        normed_rows = lax.all_gather(normed.astype(jnp.bfloat16), "gy", axis=0, tiled=True)
        cos_table, sin_table = rotary_tables(position[:, micro], query_start, query_rows)
        query_pre = (
            jnp.einsum("srd,dc->src", normed_rows, full_query, preferred_element_type=jnp.float32)
            + query_bias
        )
        key_pre = (
            jnp.einsum("srd,dc->src", normed_rows, full_key, preferred_element_type=jnp.float32)
            + key_bias
        )
        value_pre = (
            jnp.einsum("srd,dc->src", normed_rows, full_value, preferred_element_type=jnp.float32)
            + value_bias
        )
        queries = rotate(query_pre.reshape(head_shape), cos_table, sin_table).astype(jnp.bfloat16)
        key_here = rotate(key_pre.reshape(head_shape), cos_table, sin_table).astype(jnp.bfloat16)
        value_here = value_pre.reshape(head_shape).astype(jnp.bfloat16)
        keys_all, values_all = (
            lax.all_gather(key_here, "gx", axis=0, tiled=True),
            lax.all_gather(value_here, "gx", axis=0, tiled=True),
        )
        picture_row = picture[micro]
        query_picture = lax.dynamic_slice_in_dim(picture_row, query_start, query_rows, 1)
        query_places = query_start + jnp.arange(query_rows)
        same_picture = (query_picture[:, :, None] == picture_row[:, None, :]) & (
            patch_mask[micro][:, None, :] == 1
        )
        itself = (query_places[:, None] == jnp.arange(slot_count)[None, :])[None]
        visible = same_picture | itself
        scores = attention_scores(queries, keys_all, visible)
        highest = jnp.max(scores, axis=-1, keepdims=True)
        raised = jnp.exp(scores - highest)
        summed = jnp.sum(raised, axis=-1, keepdims=True)
        log_total = highest + jnp.log(summed)
        attend = (raised / summed).astype(jnp.bfloat16)
        mixture = jnp.einsum(
            "rhqk,krhd->qrhd", attend, values_all, preferred_element_type=jnp.float32
        )
        mixture = mixture.reshape(query_rows, row_count, head_cols).astype(jnp.bfloat16)
        branch = (
            lax.psum_scatter(
                jnp.einsum("srh,oh->sro", mixture, full_out, preferred_element_type=jnp.float32),
                "gy",
                scatter_dimension=0,
                tiled=True,
            )
            + b_out
        )
        middle = inputs + branch
        normed_two, normal_two, factor_two = layer_norm(middle, gain_mlp, shift_mlp)
        mlp_rows = lax.all_gather(normed_two.astype(jnp.bfloat16), "gy", axis=0, tiled=True)
        hidden = (
            jnp.einsum("srd,df->srf", mlp_rows, full_up, preferred_element_type=jnp.float32)
            + up_bias
        )
        squashed = jax.nn.sigmoid(1.702 * hidden)
        active = (hidden * squashed).astype(jnp.bfloat16)
        result = (
            lax.psum_scatter(
                jnp.einsum(
                    "srf,of->sro", active, full_down, preferred_element_type=jnp.float32
                ).astype(jnp.bfloat16),
                "gy",
                scatter_dimension=0,
                tiled=True,
            ).astype(jnp.float32)
            + b_down
        )
        outputs.append(jnp.transpose(middle + result, (1, 0, 2)).astype(jnp.bfloat16))
        cotangent = jnp.transpose(out_grad[micro], (1, 0, 2))
        sum_down_bias = sum_down_bias + jnp.sum(cotangent.astype(jnp.float32), axis=(0, 1))
        cot_rows = lax.all_gather(cotangent, "gy", axis=0, tiled=True)
        grad_down = jnp.einsum("srd,srf->df", cot_rows, active, preferred_element_type=jnp.float32)
        active_grad = jnp.einsum(
            "srd,df->srf", cot_rows, full_down, preferred_element_type=jnp.float32
        )
        hidden_grad = (
            active_grad * (squashed + 1.702 * hidden * squashed * (1.0 - squashed))
        ).astype(jnp.bfloat16)
        sum_up_bias = sum_up_bias + jnp.sum(hidden_grad.astype(jnp.float32), axis=(0, 1))
        grad_up = jnp.einsum(
            "srd,srf->df", mlp_rows, hidden_grad, preferred_element_type=jnp.float32
        )
        normed_two_grad = lax.psum_scatter(
            jnp.einsum("srf,df->srd", hidden_grad, full_up, preferred_element_type=jnp.float32),
            "gy",
            scatter_dimension=0,
            tiled=True,
        )
        sum_gain_mlp = sum_gain_mlp + jnp.sum(normed_two_grad * normal_two, axis=(0, 1))
        sum_shift_mlp = sum_shift_mlp + jnp.sum(normed_two_grad, axis=(0, 1))
        middle_grad = cotangent.astype(jnp.float32) + norm_back(
            normed_two_grad, normal_two, factor_two, gain_mlp
        )
        branch_grad = middle_grad.astype(jnp.bfloat16)
        sum_out_bias = sum_out_bias + jnp.sum(branch_grad.astype(jnp.float32), axis=(0, 1))
        branch_rows = lax.all_gather(branch_grad, "gy", axis=0, tiled=True)
        grad_out = jnp.einsum(
            "srd,srh->dh", branch_rows, mixture, preferred_element_type=jnp.float32
        )
        mixture_grad = jnp.einsum(
            "srd,dh->srh", branch_rows, full_out, preferred_element_type=jnp.float32
        )
        mixture_grad = mixture_grad.astype(jnp.bfloat16).reshape(head_shape)
        again = jnp.exp(attention_scores(queries, keys_all, visible) - log_total)
        again_low = again.astype(jnp.bfloat16)
        attend_grad = jnp.einsum(
            "qrhd,krhd->rhqk", mixture_grad, values_all, preferred_element_type=jnp.float32
        )
        score_grad = (
            again * (attend_grad - jnp.sum(again * attend_grad, axis=-1, keepdims=True))
        ).astype(jnp.bfloat16)
        query_grad = (
            jnp.einsum("rhqk,krhd->qrhd", score_grad, keys_all, preferred_element_type=jnp.float32)
            * scaling
        )
        key_part = (
            jnp.einsum("rhqk,qrhd->krhd", score_grad, queries, preferred_element_type=jnp.float32)
            * scaling
        )
        value_part = jnp.einsum(
            "rhqk,qrhd->krhd", again_low, mixture_grad, preferred_element_type=jnp.float32
        )
        key_grad, value_grad = (
            lax.psum_scatter(key_part, "gx", scatter_dimension=0, tiled=True),
            lax.psum_scatter(value_part, "gx", scatter_dimension=0, tiled=True),
        )
        flat_shape = (query_rows, row_count, head_cols)
        query_pre_grad = (
            rotate_back(query_grad, cos_table, sin_table).reshape(flat_shape).astype(jnp.bfloat16)
        )
        key_pre_grad = (
            rotate_back(key_grad, cos_table, sin_table).reshape(flat_shape).astype(jnp.bfloat16)
        )
        value_pre_grad = value_grad.reshape(flat_shape).astype(jnp.bfloat16)
        sum_query_bias = sum_query_bias + jnp.sum(query_pre_grad.astype(jnp.float32), axis=(0, 1))
        sum_key_bias = sum_key_bias + jnp.sum(key_pre_grad.astype(jnp.float32), axis=(0, 1))
        sum_value_bias = sum_value_bias + jnp.sum(value_pre_grad.astype(jnp.float32), axis=(0, 1))
        grad_query = jnp.einsum(
            "srd,src->dc", normed_rows, query_pre_grad, preferred_element_type=jnp.float32
        )
        grad_key = jnp.einsum(
            "srd,src->dc", normed_rows, key_pre_grad, preferred_element_type=jnp.float32
        )
        grad_value = jnp.einsum(
            "srd,src->dc", normed_rows, value_pre_grad, preferred_element_type=jnp.float32
        )
        from_query = jnp.einsum(
            "src,dc->srd", query_pre_grad, full_query, preferred_element_type=jnp.float32
        )
        from_key = jnp.einsum(
            "src,dc->srd", key_pre_grad, full_key, preferred_element_type=jnp.float32
        )
        from_value = jnp.einsum(
            "src,dc->srd", value_pre_grad, full_value, preferred_element_type=jnp.float32
        )
        normed_grad = lax.psum_scatter(
            (from_query + from_key + from_value).astype(jnp.bfloat16),
            "gy",
            scatter_dimension=0,
            tiled=True,
        ).astype(jnp.float32)
        sum_gain_attn = sum_gain_attn + jnp.sum(normed_grad * normal_one, axis=(0, 1))
        sum_shift_attn = sum_shift_attn + jnp.sum(normed_grad, axis=(0, 1))
        input_grad = middle_grad + norm_back(normed_grad, normal_one, factor_one, gain_attn)
        input_grads.append(jnp.transpose(input_grad, (1, 0, 2)))
        reduced = (
            lax.psum_scatter(grad_query, ("dp", "gx"), scatter_dimension=0, tiled=True),
            lax.psum_scatter(grad_key, ("dp", "gx"), scatter_dimension=0, tiled=True),
            lax.psum_scatter(grad_value, ("dp", "gx"), scatter_dimension=0, tiled=True),
            lax.psum_scatter(grad_out, ("dp", "gx"), scatter_dimension=0, tiled=True),
            lax.psum_scatter(grad_up, ("dp", "gx"), scatter_dimension=0, tiled=True),
            lax.psum_scatter(grad_down, ("dp", "gx"), scatter_dimension=0, tiled=True),
        )
        grad_shards = [held + fresh for held, fresh in zip(grad_shards, reduced)]
    query_bias_full = lax.dynamic_update_slice_in_dim(
        jnp.zeros(b_query.shape, jnp.float32), sum_query_bias, head_start, 0
    )
    key_bias_full = lax.dynamic_update_slice_in_dim(
        jnp.zeros(b_key.shape, jnp.float32), sum_key_bias, head_start, 0
    )
    value_bias_full = lax.dynamic_update_slice_in_dim(
        jnp.zeros(b_value.shape, jnp.float32), sum_value_bias, head_start, 0
    )
    up_bias_full = lax.dynamic_update_slice_in_dim(
        jnp.zeros(b_up.shape, jnp.float32), sum_up_bias, up_start, 0
    )
    vectors = lax.psum(
        (
            sum_gain_attn,
            sum_shift_attn,
            query_bias_full,
            key_bias_full,
            value_bias_full,
            sum_out_bias,
            sum_gain_mlp,
            sum_shift_mlp,
            up_bias_full,
            sum_down_bias,
        ),
        ("dp", "gx", "gy"),
    )
    block_output = jnp.stack(outputs)
    input_grad_all = jnp.stack(input_grads)
    return (
        block_output,
        input_grad_all,
        vectors[0],
        vectors[1],
        grad_shards[0],
        vectors[2],
        grad_shards[1],
        vectors[3],
        grad_shards[2],
        vectors[4],
        grad_shards[3],
        vectors[5],
        vectors[6],
        vectors[7],
        grad_shards[4],
        vectors[8],
        grad_shards[5],
        vectors[9],
    )


def solution(mesh):
    placed = (
        P(None, "dp", ("gx", "gy"), None),
        P(None, "dp", None),
        P(None, None, "dp", None),
        P(None, "dp", None),
        P(),
        P(),
        P(("dp", "gx"), "gy"),
        P(),
        P(("dp", "gx"), "gy"),
        P(),
        P(("dp", "gx"), "gy"),
        P(),
        P(("dp", "gx"), "gy"),
        P(),
        P(),
        P(),
        P(("dp", "gx"), "gy"),
        P(),
        P(("dp", "gx"), "gy"),
        P(),
        P(None, "dp", ("gx", "gy"), None),
    )
    return jax.shard_map(
        per_device,
        mesh=mesh,
        in_specs=placed,
        out_specs=(
            P(None, "dp", ("gx", "gy"), None),
            P(None, "dp", ("gx", "gy"), None),
            P(),
            P(),
            P(("dp", "gx"), "gy"),
            P(),
            P(("dp", "gx"), "gy"),
            P(),
            P(("dp", "gx"), "gy"),
            P(),
            P(("dp", "gx"), "gy"),
            P(),
            P(),
            P(),
            P(("dp", "gx"), "gy"),
            P(),
            P(("dp", "gx"), "gy"),
            P(),
        ),
        check_vma=False,
    )
```

profile of v0, /device:TPU:0, one launch (start us, length us, event | category | flops | bytes accessed | tf_op | source)
XLA Modules:
  0.0 1798.1 jit_solution(1486802666801768990)
XLA Ops:
  16.6 36.7 %all_gather.88 = bf16[1280,320]{1,0:T(8,128)(2,1)S(1)} all-gather(bf16[160,320]{1,0:T(8,128)(2,1)S(1)} %copy-done.107), channel_id=1, replica_groups=mesh['dp'=2,'gx'=4,'gy'=4] {'dp','gx'}, dimensions={0}, use_global_device_ids=true | all-gather | bytes 921600 | tf_op jit(solution)/shard_map/all_gather | solution.py:119
  57.5 36.6 %all_gather.85 = bf16[1280,320]{1,0:T(8,128)(2,1)S(1)} all-gather(bf16[160,320]{1,0:T(8,128)(2,1)S(1)} %copy-done.108), channel_id=1, replica_groups=mesh['dp'=2,'gx'=4,'gy'=4] {'dp','gx'}, dimensions={0}, use_global_device_ids=true | all-gather | bytes 921600 | tf_op jit(solution)/shard_map/all_gather | solution.py:120
  108.2 42.6 %all_gather.87 = bf16[1280,320]{1,0:T(8,128)(2,1)} all-gather(bf16[160,320]{1,0:T(8,128)(2,1)} %param.27), channel_id=1, replica_groups=mesh['dp'=2,'gx'=4,'gy'=4] {'dp','gx'}, dimensions={0}, use_global_device_ids=true | all-gather | bytes 921600 | tf_op jit(solution)/shard_map/all_gather | solution.py:118
  154.0 40.2 %all_gather.90 = bf16[1280,320]{1,0:T(8,128)(2,1)} all-gather(bf16[160,320]{1,0:T(8,128)(2,1)} %param.33), channel_id=1, replica_groups=mesh['dp'=2,'gx'=4,'gy'=4] {'dp','gx'}, dimensions={0}, use_global_device_ids=true | all-gather | bytes 921600 | tf_op jit(solution)/shard_map/all_gather | solution.py:121
  203.9 9.1 fusion.289
  213.0 8.2 fusion
  221.3 8.0 fusion.178
  234.3 9.6 fusion.291
  243.9 8.2 fusion.2
  252.1 8.0 fusion.172
  266.0 9.5 fusion.290
  275.6 8.1 fusion.1
  283.7 15.2 all-gather.38.cloned.1.call-done
  298.9 7.9 fusion.175
  309.8 25.1 %reduce-scatter.27.cloned.1.call-done = f32[128,1,1280]{2,0,1:T(8,128)} async-done(((f32[512,1,1280]{2,0,1:T(8,128)}), f32[128,1,1280]{2,0,1:T(8,128)}) %reduce-scatter.27.cloned.1.call-update) | async-done | bytes 655376 | tf_op jit(solution)/shard_map/reduce_scatter | solution.py:168
  334.9 37.1 %reduce-scatter.35.cloned.1.call-done = f32[128,1,1280]{2,0,1:T(8,128)} async-done(((f32[512,1,1280]{2,0,1:T(8,128)}), f32[128,1,1280]{2,0,1:T(8,128)}) %reduce-scatter.35.cloned.1.call-update) | async-done | bytes 655376 | tf_op jit(solution)/shard_map/reduce_scatter | solution.py:168
  372.0 36.9 %reduce-scatter.31.cloned.1.call-done = f32[128,1,1280]{2,0,1:T(8,128)} async-done(((f32[512,1,1280]{2,0,1:T(8,128)}), f32[128,1,1280]{2,0,1:T(8,128)}) %reduce-scatter.31.cloned.1.call-update) | async-done | bytes 655376 | tf_op jit(solution)/shard_map/reduce_scatter | solution.py:168
  418.3 12.6 all-gather.30.cloned.1.call-done
  436.6 13.8 all-gather.58.cloned.1.call-done
  450.4 63.4 %all-gather.34.cloned.1.call-done = bf16[1280,1280]{1,0:T(8,128)(2,1)} async-done(((bf16[160,1280]{1,0:T(8,128)(2,1)}), bf16[1280,1280]{1,0:T(8,128)(2,1)}) %all-gather.34.cloned.1.call-update) | async-done | bytes 3276816 | tf_op jit(solution)/shard_map/all_gather | solution.py:123
  524.6 8.1 all-gather.50.cloned.1.call-done
  538.4 14.0 all-gather.62.cloned.1.call-done
  563.4 9.0 all-gather.42.cloned.1.call-done
  578.2 13.8 all-gather.60.cloned.1.call-done
  628.8 37.0 %reduce-scatter.55.cloned.1.call-done = f32[128,1,1280]{2,0,1:T(8,128)} async-done(((f32[512,1,1280]{2,0,1:T(8,128)}), f32[128,1,1280]{2,0,1:T(8,128)}) %reduce-scatter.55.cloned.1.call-update) | async-done | bytes 655376 | tf_op jit(solution)/shard_map/reduce_scatter | solution.py:211
  665.7 36.8 %reduce-scatter.47.cloned.1.call-done = f32[128,1,1280]{2,0,1:T(8,128)} async-done(((f32[512,1,1280]{2,0,1:T(8,128)}), f32[128,1,1280]{2,0,1:T(8,128)}) %reduce-scatter.47.cloned.1.call-update) | async-done | bytes 655376 | tf_op jit(solution)/shard_map/reduce_scatter | solution.py:211
  705.4 26.1 %reduce-scatter.33.cloned.1.call-done = bf16[128,1,1280]{2,0,1:T(8,128)(2,1)} async-done(((bf16[512,1,1280]{2,0,1:T(8,128)(2,1)}), bf16[128,1,1280]{2,0,1:T(8,128)(2,1)}) %reduce-scatter.33.cloned.1.call-update) | async-done | bytes 327696 | tf_op jit(solution)/shard_map/reduce_scatter | solution.py:186
  735.2 25.7 %reduce-scatter.37.cloned.1.call-done = bf16[128,1,1280]{2,0,1:T(8,128)(2,1)} async-done(((bf16[512,1,1280]{2,0,1:T(8,128)(2,1)}), bf16[128,1,1280]{2,0,1:T(8,128)(2,1)}) %reduce-scatter.37.cloned.1.call-update) | async-done | bytes 327696 | tf_op jit(solution)/shard_map/reduce_scatter | solution.py:186
  760.8 28.9 %reduce-scatter.29.cloned.1.call-done = bf16[128,1,1280]{2,0,1:T(8,128)(2,1)} async-done(((bf16[512,1,1280]{2,0,1:T(8,128)(2,1)}), bf16[128,1,1280]{2,0,1:T(8,128)(2,1)}) %reduce-scatter.29.cloned.1.call-update) | async-done | bytes 327696 | tf_op jit(solution)/shard_map/reduce_scatter | solution.py:186
  797.4 14.0 multiply_reduce_fusion.1
  814.4 7.9 multiply_convert_fusion.1
  829.7 10.0 fusion.34
  843.3 13.8 multiply_reduce_fusion.2
  875.2 10.1 fusion.31
  888.8 13.8 multiply_reduce_fusion
  920.9 10.1 fusion.37
  963.2 31.7 %reduce-scatter.41.cloned.1.call-done = f32[512,1,4,80]{0,3,2,1:T(8,128)} async-done(((f32[2048,1,4,80]{0,3,2,1:T(8,128)}), f32[512,1,4,80]{0,3,2,1:T(8,128)}) %reduce-scatter.41.cloned.1.call-update) | async-done | bytes 655376 | tf_op jit(solution)/shard_map/reduce_scatter | solution.py:252
  997.0 52.1 %reduce-scatter.43.cloned.1.call-done = f32[512,1,4,80]{0,3,2,1:T(8,128)} async-done(((f32[2048,1,4,80]{0,3,2,1:T(8,128)}), f32[512,1,4,80]{0,3,2,1:T(8,128)}) %reduce-scatter.43.cloned.1.call-update) | async-done | bytes 655376 | tf_op jit(solution)/shard_map/reduce_scatter | solution.py:253
  1065.4 37.7 %reduce-scatter.57.cloned.1.call-done = f32[512,1,4,80]{0,3,2,1:T(8,128)} async-done(((f32[2048,1,4,80]{0,3,2,1:T(8,128)}), f32[512,1,4,80]{0,3,2,1:T(8,128)}) %reduce-scatter.57.cloned.1.call-update) | async-done | bytes 655376 | tf_op jit(solution)/shard_map/reduce_scatter | solution.py:252
  1105.1 52.1 %reduce-scatter.59.cloned.1.call-done = f32[512,1,4,80]{0,3,2,1:T(8,128)} async-done(((f32[2048,1,4,80]{0,3,2,1:T(8,128)}), f32[512,1,4,80]{0,3,2,1:T(8,128)}) %reduce-scatter.59.cloned.1.call-update) | async-done | bytes 655376 | tf_op jit(solution)/shard_map/reduce_scatter | solution.py:253
  1186.4 8.2 copy.41
  1215.1 28.4 %reduce-scatter.61.cloned.1.call-done = bf16[128,1,1280]{2,0,1:T(8,128)(2,1)} async-done(((bf16[512,1,1280]{2,0,1:T(8,128)(2,1)}), bf16[128,1,1280]{2,0,1:T(8,128)(2,1)}) %reduce-scatter.61.cloned.1.call-update) | async-done | bytes 327696 | tf_op jit(solution)/shard_map/reduce_scatter | solution.py:284
  1262.2 53.0 %reduce-scatter.69.cloned.1.call-done = f32[160,320]{1,0:T(8,128)} async-done(((f32[1280,320]{1,0:T(8,128)}), f32[160,320]{1,0:T(8,128)}) %reduce-scatter.69.cloned.1.call-update) | async-done | bytes 204816 | tf_op jit(solution)/shard_map/reduce_scatter | solution.py:298
  1315.2 70.8 %reduce-scatter.63.cloned.1.call-done = f32[160,320]{1,0:T(8,128)} async-done(((f32[1280,320]{1,0:T(8,128)}), f32[160,320]{1,0:T(8,128)}) %reduce-scatter.63.cloned.1.call-update) | async-done | bytes 204816 | tf_op jit(solution)/shard_map/reduce_scatter | solution.py:295
  1386.0 124.7 %reduce-scatter.73.cloned.1.call-done = f32[160,1280]{1,0:T(8,128)} async-done(((f32[1280,1280]{1,0:T(8,128)}), f32[160,1280]{1,0:T(8,128)}) %reduce-scatter.73.cloned.1.call-update) | async-done | bytes 819216
  1510.7 125.2 %reduce-scatter.71.cloned.1.call-done = f32[160,1280]{1,0:T(8,128)} async-done(((f32[1280,1280]{1,0:T(8,128)}), f32[160,1280]{1,0:T(8,128)}) %reduce-scatter.71.cloned.1.call-update) | async-done | bytes 819216 | tf_op jit(solution)/shard_map/reduce_scatter | solution.py:299
  1635.9 70.9 %reduce-scatter.67.cloned.1.call-done = f32[160,320]{1,0:T(8,128)} async-done(((f32[1280,320]{1,0:T(8,128)}), f32[160,320]{1,0:T(8,128)}) %reduce-scatter.67.cloned.1.call-update) | async-done | bytes 204816 | tf_op jit(solution)/shard_map/reduce_scatter | solution.py:297
  1706.8 70.3 %reduce-scatter.65.cloned.1.call-done = f32[160,320]{1,0:T(8,128)} async-done(((f32[1280,320]{1,0:T(8,128)}), f32[160,320]{1,0:T(8,128)}) %reduce-scatter.65.cloned.1.call-update) | async-done | bytes 204816 | tf_op jit(solution)/shard_map/reduce_scatter | solution.py:296
  (669 shorter events, 337.9 us)
Async XLA Ops:
  8.0 45.2 %all-gather.24.cloned.1.call-start = ((), (), s32[]{:S(2)}) async-start(), calls=%async_computation.24 | async-start | bytes 1638400 | tf_op jit(solution)/shard_map/all_gather | solution.py:128
  13.3 84.6 %all-gather.44.cloned.1.call-start = ((), (), s32[]{:S(2)}) async-start(), calls=%async_computation.38 | async-start | bytes 1638400 | tf_op jit(solution)/shard_map/all_gather | solution.py:128
  14.1 136.8 %all-gather.36.cloned.1.call-start = ((), (), s32[]{:S(2)}) async-start(), calls=%async_computation.32 | async-start | bytes 1638400 | tf_op jit(solution)/shard_map/all_gather | solution.py:128
  14.8 189.1 %all-gather.28.cloned.1.call-start = ((), (), s32[]{:S(2)}) async-start(), calls=%async_computation.26 | async-start | bytes 1638400 | tf_op jit(solution)/shard_map/all_gather | solution.py:146
  56.7 164.6 %all-gather.26.cloned.1.call-start = ((), (), s32[]{:S(2)}) async-start(), calls=%async_computation.25 | async-start | bytes 1638400 | tf_op jit(solution)/shard_map/all_gather | solution.py:147
  94.1 106.5 %copy-start.7 = (bf16[1280,320]{1,0:T(8,128)(2,1)}, bf16[1280,320]{1,0:T(8,128)(2,1)S(1)}, u32[]{:S(2)}) copy-start(bf16[1280,320]{1,0:T(8,128)(2,1)S(1)} %all_gather.85) | copy-start | bytes 2457604
  97.2 137.1 %all-gather.48.cloned.1.call-start = ((), (), s32[]{:S(2)}) async-start(), calls=%async_computation.40 | async-start | bytes 1638400 | tf_op jit(solution)/shard_map/all_gather | solution.py:146
  97.9 136.2 %copy-start.58 = (f32[512,80]{0,1:T(8,128)}, f32[512,80]{0,1:T(8,128)S(1)}, u32[]{:S(2)}) copy-start(f32[512,80]{0,1:T(8,128)S(1)} %get-tuple-element.189) | copy-start | bytes 491524
  101.0 151.1 %all-gather.46.cloned.1.call-start = ((), (), s32[]{:S(2)}) async-start(), calls=%async_computation.39 | async-start | bytes 1638400 | tf_op jit(solution)/shard_map/all_gather | solution.py:147
  105.7 160.3 %all-gather.40.cloned.1.call-start = ((), (), s32[]{:S(2)}) async-start(), calls=%async_computation.34 | async-start | bytes 1638400 | tf_op jit(solution)/shard_map/all_gather | solution.py:146
  154.0 144.9 %all-gather.38.cloned.1.call-start = ((), (), s32[]{:S(2)}) async-start(), calls=%async_computation.33 | async-start | bytes 1638400 | tf_op jit(solution)/shard_map/all_gather | solution.py:147
  202.0 132.9 %reduce-scatter.27.cloned.1.call-start = ((), (), s32[]{:S(2)}) async-start(), calls=%async_computation.27 | async-start | bytes 3276800 | tf_op jit(solution)/shard_map/reduce_scatter | solution.py:168
  231.7 140.3 %reduce-scatter.35.cloned.1.call-start = ((), (), s32[]{:S(2)}) async-start(), calls=%async_computation.41 | async-start | bytes 3276800 | tf_op jit(solution)/shard_map/reduce_scatter | solution.py:168
  263.3 145.7 %reduce-scatter.31.cloned.1.call-start = ((), (), s32[]{:S(2)}) async-start(), calls=%async_computation.35 | async-start | bytes 3276800 | tf_op jit(solution)/shard_map/reduce_scatter | solution.py:168
  309.2 109.1 %all-gather.32.cloned.1.call-start = ((), (), s32[]{:S(2)}) async-start(), calls=%async_computation.29 | async-start | bytes 3686400 | tf_op jit(solution)/shard_map/all_gather | solution.py:122
  309.8 121.1 %all-gather.30.cloned.1.call-start = ((), (), s32[]{:S(2)}) async-start(), calls=%async_computation.28 | async-start | bytes 1638400 | tf_op jit(solution)/shard_map/all_gather | solution.py:178
  412.8 37.6 %all-gather.58.cloned.1.call-start = ((), (), s32[]{:S(2)}) async-start(), calls=%async_computation.59 | async-start | bytes 1638400 | tf_op jit(solution)/shard_map/all_gather | solution.py:199
  413.8 100.0 %all-gather.34.cloned.1.call-start = ((), (), s32[]{:S(2)}) async-start(), calls=%async_computation.30 | async-start | bytes 3686400 | tf_op jit(solution)/shard_map/all_gather | solution.py:123
  414.6 118.1 %all-gather.50.cloned.1.call-start = ((), (), s32[]{:S(2)}) async-start(), calls=%async_computation.42 | async-start | bytes 1638400 | tf_op jit(solution)/shard_map/all_gather | solution.py:178
  415.3 137.0 %all-gather.62.cloned.1.call-start = ((), (), s32[]{:S(2)}) async-start(), calls=%async_computation.61 | async-start | bytes 1638400 | tf_op jit(solution)/shard_map/all_gather | solution.py:199
  416.1 156.4 %all-gather.42.cloned.1.call-start = ((), (), s32[]{:S(2)}) async-start(), calls=%async_computation.36 | async-start | bytes 1638400 | tf_op jit(solution)/shard_map/all_gather | solution.py:178
  416.7 175.3 %all-gather.60.cloned.1.call-start = ((), (), s32[]{:S(2)}) async-start(), calls=%async_computation.60 | async-start | bytes 1638400 | tf_op jit(solution)/shard_map/all_gather | solution.py:199
  417.2 211.5 %reduce-scatter.39.cloned.1.call-start = ((), (), s32[]{:S(2)}) async-start(), calls=%async_computation.44 | async-start | bytes 3276800 | tf_op jit(solution)/shard_map/reduce_scatter | solution.py:211
  524.5 141.2 %reduce-scatter.55.cloned.1.call-start = ((), (), s32[]{:S(2)}) async-start(), calls=%async_computation.54 | async-start | bytes 3276800 | tf_op jit(solution)/shard_map/reduce_scatter | solution.py:211
  563.1 139.4 %reduce-scatter.47.cloned.1.call-start = ((), (), s32[]{:S(2)}) async-start(), calls=%async_computation.49 | async-start | bytes 3276800 | tf_op jit(solution)/shard_map/reduce_scatter | solution.py:211
  602.7 128.7 %reduce-scatter.33.cloned.1.call-start = ((), (), s32[]{:S(2)}) async-start(), calls=%async_computation.37 | async-start | bytes 1638400 | tf_op jit(solution)/shard_map/reduce_scatter | solution.py:186
  609.0 151.9 %reduce-scatter.37.cloned.1.call-start = ((), (), s32[]{:S(2)}) async-start(), calls=%async_computation.43 | async-start | bytes 1638400 | tf_op jit(solution)/shard_map/reduce_scatter | solution.py:186
  615.2 174.6 %reduce-scatter.29.cloned.1.call-start = ((), (), s32[]{:S(2)}) async-start(), calls=%async_computation.31 | async-start | bytes 1638400 | tf_op jit(solution)/shard_map/reduce_scatter | solution.py:186
  621.3 110.2 %copy-start.121 = (f32[1280]{0:T(1024)S(1)}, f32[1280]{0:T(1024)}, u32[]{:S(2)}) copy-start(f32[1280]{0:T(1024)} %param.40) | copy-start | bytes 15364
  621.3 173.4 %all-gather.54.cloned.1.call-start = ((), (), s32[]{:S(2)}) async-start(), calls=%async_computation.50 | async-start | bytes 1638400 | tf_op jit(solution)/shard_map/all_gather | solution.py:224
  734.7 105.8 %all-gather.52.cloned.1.call-start = ((), (), s32[]{:S(2)}) async-start(), calls=%async_computation.45 | async-start | bytes 1638400 | tf_op jit(solution)/shard_map/all_gather | solution.py:224
  794.0 92.1 %all-gather.56.cloned.1.call-start = ((), (), s32[]{:S(2)}) async-start(), calls=%async_computation.55 | async-start | bytes 1638400 | tf_op jit(solution)/shard_map/all_gather | solution.py:224
  794.6 150.2 %reduce-scatter.49.cloned.1.call-start = ((), (), s32[]{:S(2)}) async-start(), calls=%async_computation.51 | async-start | bytes 3276800 | tf_op jit(solution)/shard_map/reduce_scatter | solution.py:252
  828.7 118.1 %reduce-scatter.51.cloned.1.call-start = ((), (), s32[]{:S(2)}) async-start(), calls=%async_computation.52 | async-start | bytes 3276800 | tf_op jit(solution)/shard_map/reduce_scatter | solution.py:253
  839.8 155.2 %reduce-scatter.41.cloned.1.call-start = ((), (), s32[]{:S(2)}) async-start(), calls=%async_computation.46 | async-start | bytes 3276800 | tf_op jit(solution)/shard_map/reduce_scatter | solution.py:252
  874.3 174.8 %reduce-scatter.43.cloned.1.call-start = ((), (), s32[]{:S(2)}) async-start(), calls=%async_computation.47 | async-start | bytes 3276800 | tf_op jit(solution)/shard_map/reduce_scatter | solution.py:253
  885.4 217.7 %reduce-scatter.57.cloned.1.call-start = ((), (), s32[]{:S(2)}) async-start(), calls=%async_computation.56 | async-start | bytes 3276800 | tf_op jit(solution)/shard_map/reduce_scatter | solution.py:252
  920.0 237.2 %reduce-scatter.59.cloned.1.call-start = ((), (), s32[]{:S(2)}) async-start(), calls=%async_computation.57 | async-start | bytes 3276800 | tf_op jit(solution)/shard_map/reduce_scatter | solution.py:253
  931.1 284.0 %reduce-scatter.53.cloned.1.call-start = ((), (), s32[]{:S(2)}) async-start(), calls=%async_computation.53 | async-start | bytes 1638400 | tf_op jit(solution)/shard_map/reduce_scatter | solution.py:284
  952.9 262.2 %reduce-scatter.45.cloned.1.call-start = ((), (), s32[]{:S(2)}) async-start(), calls=%async_computation.48 | async-start | bytes 1638400 | tf_op jit(solution)/shard_map/reduce_scatter | solution.py:284
  1055.0 188.6 %reduce-scatter.61.cloned.1.call-start = ((), (), s32[]{:S(2)}) async-start(), calls=%async_computation.58 | async-start | bytes 1638400 | tf_op jit(solution)/shard_map/reduce_scatter | solution.py:284
  1163.2 152.0 %reduce-scatter.69.cloned.1.call-start = ((), (), s32[]{:S(2)}) async-start(), calls=%async_computation.65 | async-start | bytes 2211840 | tf_op jit(solution)/shard_map/reduce_scatter | solution.py:298
  1169.6 216.4 %reduce-scatter.63.cloned.1.call-start = ((), (), s32[]{:S(2)}) async-start(), calls=%async_computation.62 | async-start | bytes 2211840 | tf_op jit(solution)/shard_map/reduce_scatter | solution.py:295
  1175.1 335.5 %reduce-scatter.73.cloned.1.call-start = ((), (), s32[]{:S(2)}) async-start(), calls=%async_computation.67 | async-start | bytes 7372800
  1194.6 441.3 %reduce-scatter.71.cloned.1.call-start = ((), (), s32[]{:S(2)}) async-start(), calls=%async_computation.66 | async-start | bytes 7372800 | tf_op jit(solution)/shard_map/reduce_scatter | solution.py:299
  1205.6 430.2 %all-reduce.3.cloned.1.call-start = ((), (), s32[]{:S(2)}) async-start(), calls=%async_computation.68 | async-start | bytes 188416 | tf_op jit(solution)/shard_map/psum | solution.py:315
  1247.0 459.8 %reduce-scatter.67.cloned.1.call-start = ((), (), s32[]{:S(2)}) async-start(), calls=%async_computation.64 | async-start | bytes 2211840 | tf_op jit(solution)/shard_map/reduce_scatter | solution.py:297
  1251.2 525.9 %reduce-scatter.65.cloned.1.call-start = ((), (), s32[]{:S(2)}) async-start(), calls=%async_computation.63 | async-start | bytes 2211840 | tf_op jit(solution)/shard_map/reduce_scatter | solution.py:296
  (181 other events, 2819.1 us)
Sparse Core Ops, SparseCore 0:
  13.4 20.8 all-gather.23
  36.5 18.1 all-gather.43
  56.8 18.1 all-gather.35
  76.4 38.0 all-gather.27
  115.9 43.1 all-gather.25
  160.6 37.9 all-gather.47
  200.2 32.1 all-gather.45
  233.9 31.7 all-gather.39
  267.3 31.5 all-gather.37
  301.3 33.6 reduce-scatter.26
  337.5 34.4 reduce-scatter.34
  374.4 34.4 reduce-scatter.30
  734.8 18.1 all-gather.53
  794.1 18.1 all-gather.51
  814.3 18.1 all-gather.55
  834.7 52.2 reduce-scatter.48
  889.1 51.7 reduce-scatter.50
  943.1 51.7 reduce-scatter.40
  997.2 51.7 reduce-scatter.42
  1051.2 51.7 reduce-scatter.56
  1105.4 51.7 reduce-scatter.58
  1159.7 25.9 reduce-scatter.52
  1188.3 26.4 reduce-scatter.44
  1217.1 26.3 reduce-scatter.60
  1247.6 67.5 reduce-scatter.68
  1319.1 66.8 reduce-scatter.62
  1390.0 120.6 reduce-scatter.72
  1514.9 120.9 reduce-scatter.70
  1639.9 66.8 reduce-scatter.66
  1710.7 66.3 reduce-scatter.64
Sparse Core Ops, SparseCore 1:
  311.8 60.4 all-gather.31
  412.8 18.0 all-gather.29
  432.3 18.0 all-gather.57
  452.5 61.3 all-gather.33
  516.0 16.7 all-gather.49
  534.3 18.0 all-gather.61
  554.4 18.0 all-gather.41
  573.9 18.0 all-gather.59
  594.3 34.4 reduce-scatter.38
  631.3 34.4 reduce-scatter.54
  668.1 34.3 reduce-scatter.46
  705.1 26.3 reduce-scatter.32
  734.4 26.3 reduce-scatter.36
  763.4 26.3 reduce-scatter.28
  1247.1 138.3 all-reduce.2
where the time goes:
time: 1810 us; the launch traced here: 1800 us
  waiting for transfers between devices  1130 us (62%)
  matrix products  311 us (17%)
  blocking collectives  156 us (9%)
  other arithmetic  111 us (6%)
  local copies, waits for them, and re-layouts  61.2 us (3%)
  between operations  19.2 us (1%)
    unnamed x46, waiting for transfers between devices  131 us
    reduce_scatter x1, waiting for transfers between devices, per_device(): lax.psum_scatter(grad_up, ('dp', 'gx'), scatter_dimension=0, tiled=True)  125 us
    reduce_scatter x3, waiting for transfers between devices, per_device(): lax.psum_scatter(value_part, 'gx', scatter_dimension=0, tiled=True)  104 us
    reduce_scatter x3, waiting for transfers between devices, per_device(): lax.psum_scatter(jnp.einsum('srh,oh->sro', mixture, full_out, preferred_e...  99.1 us
    reduce_scatter x3, waiting for transfers between devices, per_device(): lax.psum_scatter(jnp.einsum('srf,df->srd', hidden_grad, full_up, preferre...  81.2 us
    reduce_scatter x3, waiting for transfers between devices, per_device(): lax.psum_scatter(jnp.einsum('srf,of->sro', active, full_down, preferred_e...  80.7 us
    reduce_scatter x1, waiting for transfers between devices, per_device(): lax.psum_scatter(grad_value, ('dp', 'gx'), scatter_dimension=0, tiled=True)  70.9 us
    reduce_scatter x1, waiting for transfers between devices, per_device(): lax.psum_scatter(grad_query, ('dp', 'gx'), scatter_dimension=0, tiled=True)  70.8 us
  transfers between devices with their start and end apart: 45, of which 28 were waited for; matrix products, arithmetic and copies ran while one was open for 24% of the time, Pallas kernels for 0%

commit v1 on v0

--- a/solution.py
+++ b/solution.py
@@ -5,6 +5,19 @@
 
 HEAD_DIM = 80
 EPSILON = 1e-06
+
+
+def ring_gather(shard, axis, dim):
+    length, index, extent = (lax.axis_size(axis), lax.axis_index(axis), shard.shape[dim])
+    right = [(i, (i + 1) % length) for i in range(length)]
+    result = jnp.zeros((*shard.shape[:dim], length * extent, *shard.shape[dim + 1 :]), shard.dtype)
+    held = shard
+    for lap in range(length):
+        owner = (index - lap) % length
+        result = lax.dynamic_update_slice_in_dim(result, held, owner * extent, axis=dim)
+        if lap < length - 1:
+            held = lax.ppermute(held, axis, right)
+    return result
 
 
 def layer_norm(values, norm_gain, norm_shift):
@@ -117,7 +130,7 @@
         blocks = (
             lax.all_gather(w_query, ("dp", "gx"), axis=0, tiled=True),
             lax.all_gather(w_key, ("dp", "gx"), axis=0, tiled=True),
-            lax.all_gather(w_value, ("dp", "gx"), axis=0, tiled=True),
+            ring_gather(w_value, ("dp", "gx"), 0),
             lax.all_gather(w_out, ("dp", "gx"), axis=0, tiled=True),
             lax.all_gather(w_up, ("dp", "gx"), axis=0, tiled=True),
             lax.all_gather(w_down, ("dp", "gx"), axis=0, tiled=True),

time: 1810 us -> 1820 us (level)
  waiting for transfers between devices: 1130 us -> 1180 us
  blocking collectives: 156 us -> 120 us
    ppermute x0 -> x7, waiting for transfers between devices: none -> 57.3 us  [ring_gather(): held = lax.ppermute(held, axis, right)]
    all_gather x1 -> x0, blocking collectives: 36.6 us -> none  [per_device(): lax.all_gather(w_value, ('dp', 'gx'), axis=0, tiled=True)]
    unnamed x379 -> x383, local copies, waits for them, and re-layouts: 54.4 us -> 55.6 us
  transfers between devices with their start and end apart: 45 -> 52, of which waited for: 28 -> 35; matrix products, arithmetic and copies ran while one was open for 24% -> 24% of each run, Pallas kernels for 0% -> 0%
where the time goes in v1:
time: 1820 us; the launch traced here: 1810 us
  waiting for transfers between devices  1180 us (65%)
  matrix products  311 us (17%)
  blocking collectives  120 us (7%)
  other arithmetic  112 us (6%)
  local copies, waits for them, and re-layouts  62.7 us (3%)
  between operations  18.9 us (1%)
    unnamed x46, waiting for transfers between devices  131 us
    reduce_scatter x1, waiting for transfers between devices, per_device(): lax.psum_scatter(grad_up, ('dp', 'gx'), scatter_dimension=0, tiled=True)  125 us
    reduce_scatter x3, waiting for transfers between devices, per_device(): lax.psum_scatter(value_part, 'gx', scatter_dimension=0, tiled=True)  104 us
    reduce_scatter x3, waiting for transfers between devices, per_device(): lax.psum_scatter(jnp.einsum('srh,oh->sro', mixture, full_out, preferred_e...  99 us
    reduce_scatter x3, waiting for transfers between devices, per_device(): lax.psum_scatter(jnp.einsum('srf,df->srd', hidden_grad, full_up, preferre...  81.2 us
    reduce_scatter x3, waiting for transfers between devices, per_device(): lax.psum_scatter(jnp.einsum('srf,of->sro', active, full_down, preferred_e...  80.8 us
    reduce_scatter x1, waiting for transfers between devices, per_device(): lax.psum_scatter(grad_value, ('dp', 'gx'), scatter_dimension=0, tiled=True)  70.9 us
    reduce_scatter x1, waiting for transfers between devices, per_device(): lax.psum_scatter(grad_query, ('dp', 'gx'), scatter_dimension=0, tiled=True)  70.8 us
  transfers between devices with their start and end apart: 52, of which 35 were waited for; matrix products, arithmetic and copies ran while one was open for 24% of the time, Pallas kernels for 0%

profile of v1, /device:TPU:0, one launch (start us, length us, event | category | flops | bytes accessed | tf_op | source)
XLA Modules:
  0.0 1808.9 jit_solution(3221076875394601054)
XLA Ops:
  17.8 36.7 %all_gather.82 = bf16[1280,320]{1,0:T(8,128)(2,1)S(1)} all-gather(bf16[160,320]{1,0:T(8,128)(2,1)S(1)} %copy-done.108), channel_id=1, replica_groups=mesh['dp'=2,'gx'=4,'gy'=4] {'dp','gx'}, dimensions={0}, use_global_device_ids=true | all-gather | bytes 921600 | tf_op jit(solution)/shard_map/all_gather | solution.py:132
  89.2 10.4 collective-permute-done.4
  99.6 10.3 collective-permute-done.5
  131.6 41.9 %all_gather.81 = bf16[1280,320]{1,0:T(8,128)(2,1)} all-gather(bf16[160,320]{1,0:T(8,128)(2,1)} %param.27), channel_id=1, replica_groups=mesh['dp'=2,'gx'=4,'gy'=4] {'dp','gx'}, dimensions={0}, use_global_device_ids=true | all-gather | bytes 921600 | tf_op jit(solution)/shard_map/all_gather | solution.py:131
  176.7 41.5 %all_gather.84 = bf16[1280,320]{1,0:T(8,128)(2,1)} all-gather(bf16[160,320]{1,0:T(8,128)(2,1)} %param.33), channel_id=1, replica_groups=mesh['dp'=2,'gx'=4,'gy'=4] {'dp','gx'}, dimensions={0}, use_global_device_ids=true | all-gather | bytes 921600 | tf_op jit(solution)/shard_map/all_gather | solution.py:134
  227.7 9.1 fusion.289
  236.8 8.1 fusion
  245.0 8.0 fusion.178
  259.1 9.4 fusion.291
  268.5 8.2 fusion.2
  276.7 7.9 fusion.172
  290.3 9.3 fusion.290
  299.6 8.2 fusion.1
  309.8 7.9 fusion.175
  320.8 25.1 %reduce-scatter.27.cloned.1.call-done = f32[128,1,1280]{2,0,1:T(8,128)} async-done(((f32[512,1,1280]{2,0,1:T(8,128)}), f32[128,1,1280]{2,0,1:T(8,128)}) %reduce-scatter.27.cloned.1.call-update) | async-done | bytes 655376 | tf_op jit(solution)/shard_map/reduce_scatter | solution.py:181
  345.9 37.1 %reduce-scatter.35.cloned.1.call-done = f32[128,1,1280]{2,0,1:T(8,128)} async-done(((f32[512,1,1280]{2,0,1:T(8,128)}), f32[128,1,1280]{2,0,1:T(8,128)}) %reduce-scatter.35.cloned.1.call-update) | async-done | bytes 655376 | tf_op jit(solution)/shard_map/reduce_scatter | solution.py:181
  382.9 36.9 %reduce-scatter.31.cloned.1.call-done = f32[128,1,1280]{2,0,1:T(8,128)} async-done(((f32[512,1,1280]{2,0,1:T(8,128)}), f32[128,1,1280]{2,0,1:T(8,128)}) %reduce-scatter.31.cloned.1.call-update) | async-done | bytes 655376 | tf_op jit(solution)/shard_map/reduce_scatter | solution.py:181
  429.2 12.6 all-gather.30.cloned.1.call-done
  447.5 13.8 all-gather.58.cloned.1.call-done
  461.3 63.4 %all-gather.34.cloned.1.call-done = bf16[1280,1280]{1,0:T(8,128)(2,1)} async-done(((bf16[160,1280]{1,0:T(8,128)(2,1)}), bf16[1280,1280]{1,0:T(8,128)(2,1)}) %all-gather.34.cloned.1.call-update) | async-done | bytes 3276816 | tf_op jit(solution)/shard_map/all_gather | solution.py:136
  535.5 8.2 all-gather.50.cloned.1.call-done
  549.3 14.0 all-gather.62.cloned.1.call-done
  574.5 8.8 all-gather.42.cloned.1.call-done
  589.1 13.8 all-gather.60.cloned.1.call-done
  639.6 37.0 %reduce-scatter.55.cloned.1.call-done = f32[128,1,1280]{2,0,1:T(8,128)} async-done(((f32[512,1,1280]{2,0,1:T(8,128)}), f32[128,1,1280]{2,0,1:T(8,128)}) %reduce-scatter.55.cloned.1.call-update) | async-done | bytes 655376 | tf_op jit(solution)/shard_map/reduce_scatter | solution.py:224
  676.6 36.8 %reduce-scatter.47.cloned.1.call-done = f32[128,1,1280]{2,0,1:T(8,128)} async-done(((f32[512,1,1280]{2,0,1:T(8,128)}), f32[128,1,1280]{2,0,1:T(8,128)}) %reduce-scatter.47.cloned.1.call-update) | async-done | bytes 655376 | tf_op jit(solution)/shard_map/reduce_scatter | solution.py:224
  716.4 26.1 %reduce-scatter.33.cloned.1.call-done = bf16[128,1,1280]{2,0,1:T(8,128)(2,1)} async-done(((bf16[512,1,1280]{2,0,1:T(8,128)(2,1)}), bf16[128,1,1280]{2,0,1:T(8,128)(2,1)}) %reduce-scatter.33.cloned.1.call-update) | async-done | bytes 327696 | tf_op jit(solution)/shard_map/reduce_scatter | solution.py:199
  745.9 25.9 %reduce-scatter.37.cloned.1.call-done = bf16[128,1,1280]{2,0,1:T(8,128)(2,1)} async-done(((bf16[512,1,1280]{2,0,1:T(8,128)(2,1)}), bf16[128,1,1280]{2,0,1:T(8,128)(2,1)}) %reduce-scatter.37.cloned.1.call-update) | async-done | bytes 327696 | tf_op jit(solution)/shard_map/reduce_scatter | solution.py:199
  771.8 28.9 %reduce-scatter.29.cloned.1.call-done = bf16[128,1,1280]{2,0,1:T(8,128)(2,1)} async-done(((bf16[512,1,1280]{2,0,1:T(8,128)(2,1)}), bf16[128,1,1280]{2,0,1:T(8,128)(2,1)}) %reduce-scatter.29.cloned.1.call-update) | async-done | bytes 327696 | tf_op jit(solution)/shard_map/reduce_scatter | solution.py:199
  808.3 14.0 multiply_reduce_fusion.1
  825.3 7.9 multiply_convert_fusion.1
  840.6 10.0 fusion.34
  854.3 13.8 multiply_reduce_fusion.2
  886.2 10.1 fusion.31
  899.8 13.8 multiply_reduce_fusion
  932.0 10.0 fusion.37
  974.0 31.9 %reduce-scatter.41.cloned.1.call-done = f32[512,1,4,80]{0,3,2,1:T(8,128)} async-done(((f32[2048,1,4,80]{0,3,2,1:T(8,128)}), f32[512,1,4,80]{0,3,2,1:T(8,128)}) %reduce-scatter.41.cloned.1.call-update) | async-done | bytes 655376 | tf_op jit(solution)/shard_map/reduce_scatter | solution.py:265
  1007.9 52.1 %reduce-scatter.43.cloned.1.call-done = f32[512,1,4,80]{0,3,2,1:T(8,128)} async-done(((f32[2048,1,4,80]{0,3,2,1:T(8,128)}), f32[512,1,4,80]{0,3,2,1:T(8,128)}) %reduce-scatter.43.cloned.1.call-update) | async-done | bytes 655376 | tf_op jit(solution)/shard_map/reduce_scatter | solution.py:266
  1076.3 37.7 %reduce-scatter.57.cloned.1.call-done = f32[512,1,4,80]{0,3,2,1:T(8,128)} async-done(((f32[2048,1,4,80]{0,3,2,1:T(8,128)}), f32[512,1,4,80]{0,3,2,1:T(8,128)}) %reduce-scatter.57.cloned.1.call-update) | async-done | bytes 655376 | tf_op jit(solution)/shard_map/reduce_scatter | solution.py:265
  1116.0 52.1 %reduce-scatter.59.cloned.1.call-done = f32[512,1,4,80]{0,3,2,1:T(8,128)} async-done(((f32[2048,1,4,80]{0,3,2,1:T(8,128)}), f32[512,1,4,80]{0,3,2,1:T(8,128)}) %reduce-scatter.59.cloned.1.call-update) | async-done | bytes 655376 | tf_op jit(solution)/shard_map/reduce_scatter | solution.py:266
  1197.5 8.2 copy.41
  1226.3 28.1 %reduce-scatter.61.cloned.1.call-done = bf16[128,1,1280]{2,0,1:T(8,128)(2,1)} async-done(((bf16[512,1,1280]{2,0,1:T(8,128)(2,1)}), bf16[128,1,1280]{2,0,1:T(8,128)(2,1)}) %reduce-scatter.61.cloned.1.call-update) | async-done | bytes 327696 | tf_op jit(solution)/shard_map/reduce_scatter | solution.py:297
  1272.9 53.2 %reduce-scatter.69.cloned.1.call-done = f32[160,320]{1,0:T(8,128)} async-done(((f32[1280,320]{1,0:T(8,128)}), f32[160,320]{1,0:T(8,128)}) %reduce-scatter.69.cloned.1.call-update) | async-done | bytes 204816 | tf_op jit(solution)/shard_map/reduce_scatter | solution.py:311
  1326.0 70.8 %reduce-scatter.63.cloned.1.call-done = f32[160,320]{1,0:T(8,128)} async-done(((f32[1280,320]{1,0:T(8,128)}), f32[160,320]{1,0:T(8,128)}) %reduce-scatter.63.cloned.1.call-update) | async-done | bytes 204816 | tf_op jit(solution)/shard_map/reduce_scatter | solution.py:308
  1396.9 124.7 %reduce-scatter.73.cloned.1.call-done = f32[160,1280]{1,0:T(8,128)} async-done(((f32[1280,1280]{1,0:T(8,128)}), f32[160,1280]{1,0:T(8,128)}) %reduce-scatter.73.cloned.1.call-update) | async-done | bytes 819216
  1521.6 125.2 %reduce-scatter.71.cloned.1.call-done = f32[160,1280]{1,0:T(8,128)} async-done(((f32[1280,1280]{1,0:T(8,128)}), f32[160,1280]{1,0:T(8,128)}) %reduce-scatter.71.cloned.1.call-update) | async-done | bytes 819216 | tf_op jit(solution)/shard_map/reduce_scatter | solution.py:312
  1646.8 70.9 %reduce-scatter.67.cloned.1.call-done = f32[160,320]{1,0:T(8,128)} async-done(((f32[1280,320]{1,0:T(8,128)}), f32[160,320]{1,0:T(8,128)}) %reduce-scatter.67.cloned.1.call-update) | async-done | bytes 204816 | tf_op jit(solution)/shard_map/reduce_scatter | solution.py:310
  1717.7 70.4 %reduce-scatter.65.cloned.1.call-done = f32[160,320]{1,0:T(8,128)} async-done(((f32[1280,320]{1,0:T(8,128)}), f32[160,320]{1,0:T(8,128)}) %reduce-scatter.65.cloned.1.call-update) | async-done | bytes 204816 | tf_op jit(solution)/shard_map/reduce_scatter | solution.py:309
  (695 shorter events, 379.8 us)
Async XLA Ops:
  8.0 46.4 %all-gather.24.cloned.1.call-start = ((), (), s32[]{:S(2)}) async-start(), calls=%async_computation.24 | async-start | bytes 1638400 | tf_op jit(solution)/shard_map/all_gather | solution.py:141
  13.3 108.0 %all-gather.44.cloned.1.call-start = ((), (), s32[]{:S(2)}) async-start(), calls=%async_computation.38 | async-start | bytes 1638400 | tf_op jit(solution)/shard_map/all_gather | solution.py:141
  14.1 159.5 %all-gather.36.cloned.1.call-start = ((), (), s32[]{:S(2)}) async-start(), calls=%async_computation.32 | async-start | bytes 1638400 | tf_op jit(solution)/shard_map/all_gather | solution.py:141
  14.8 212.9 %all-gather.28.cloned.1.call-start = ((), (), s32[]{:S(2)}) async-start(), calls=%async_computation.26 | async-start | bytes 1638400 | tf_op jit(solution)/shard_map/all_gather | solution.py:159
  57.8 187.1 %all-gather.26.cloned.1.call-start = ((), (), s32[]{:S(2)}) async-start(), calls=%async_computation.25 | async-start | bytes 1638400 | tf_op jit(solution)/shard_map/all_gather | solution.py:160
  57.9 8.4 collective-permute-start
  89.2 10.4 collective-permute-start.4
  99.6 10.3 collective-permute-start.5
  120.6 138.5 %all-gather.48.cloned.1.call-start = ((), (), s32[]{:S(2)}) async-start(), calls=%async_computation.40 | async-start | bytes 1638400 | tf_op jit(solution)/shard_map/all_gather | solution.py:159
  124.3 152.3 %all-gather.46.cloned.1.call-start = ((), (), s32[]{:S(2)}) async-start(), calls=%async_computation.39 | async-start | bytes 1638400 | tf_op jit(solution)/shard_map/all_gather | solution.py:160
  129.1 161.2 %all-gather.40.cloned.1.call-start = ((), (), s32[]{:S(2)}) async-start(), calls=%async_computation.34 | async-start | bytes 1638400 | tf_op jit(solution)/shard_map/all_gather | solution.py:159
  176.7 133.2 %all-gather.38.cloned.1.call-start = ((), (), s32[]{:S(2)}) async-start(), calls=%async_computation.33 | async-start | bytes 1638400 | tf_op jit(solution)/shard_map/all_gather | solution.py:160
  226.0 119.9 %reduce-scatter.27.cloned.1.call-start = ((), (), s32[]{:S(2)}) async-start(), calls=%async_computation.27 | async-start | bytes 3276800 | tf_op jit(solution)/shard_map/reduce_scatter | solution.py:181
  256.2 126.8 %reduce-scatter.35.cloned.1.call-start = ((), (), s32[]{:S(2)}) async-start(), calls=%async_computation.41 | async-start | bytes 3276800 | tf_op jit(solution)/shard_map/reduce_scatter | solution.py:181
  287.8 132.1 %reduce-scatter.31.cloned.1.call-start = ((), (), s32[]{:S(2)}) async-start(), calls=%async_computation.35 | async-start | bytes 3276800 | tf_op jit(solution)/shard_map/reduce_scatter | solution.py:181
  320.2 109.1 %all-gather.32.cloned.1.call-start = ((), (), s32[]{:S(2)}) async-start(), calls=%async_computation.29 | async-start | bytes 3686400 | tf_op jit(solution)/shard_map/all_gather | solution.py:135
  320.8 121.1 %all-gather.30.cloned.1.call-start = ((), (), s32[]{:S(2)}) async-start(), calls=%async_computation.28 | async-start | bytes 1638400 | tf_op jit(solution)/shard_map/all_gather | solution.py:191
  423.7 37.6 %all-gather.58.cloned.1.call-start = ((), (), s32[]{:S(2)}) async-start(), calls=%async_computation.59 | async-start | bytes 1638400 | tf_op jit(solution)/shard_map/all_gather | solution.py:212
  424.8 100.0 %all-gather.34.cloned.1.call-start = ((), (), s32[]{:S(2)}) async-start(), calls=%async_computation.30 | async-start | bytes 3686400 | tf_op jit(solution)/shard_map/all_gather | solution.py:136
  425.5 118.1 %all-gather.50.cloned.1.call-start = ((), (), s32[]{:S(2)}) async-start(), calls=%async_computation.42 | async-start | bytes 1638400 | tf_op jit(solution)/shard_map/all_gather | solution.py:191
  426.3 137.0 %all-gather.62.cloned.1.call-start = ((), (), s32[]{:S(2)}) async-start(), calls=%async_computation.61 | async-start | bytes 1638400 | tf_op jit(solution)/shard_map/all_gather | solution.py:212
  427.0 156.4 %all-gather.42.cloned.1.call-start = ((), (), s32[]{:S(2)}) async-start(), calls=%async_computation.36 | async-start | bytes 1638400 | tf_op jit(solution)/shard_map/all_gather | solution.py:191
  427.6 175.3 %all-gather.60.cloned.1.call-start = ((), (), s32[]{:S(2)}) async-start(), calls=%async_computation.60 | async-start | bytes 1638400 | tf_op jit(solution)/shard_map/all_gather | solution.py:212
  428.2 211.4 %reduce-scatter.39.cloned.1.call-start = ((), (), s32[]{:S(2)}) async-start(), calls=%async_computation.44 | async-start | bytes 3276800 | tf_op jit(solution)/shard_map/reduce_scatter | solution.py:224
  535.4 141.2 %reduce-scatter.55.cloned.1.call-start = ((), (), s32[]{:S(2)}) async-start(), calls=%async_computation.54 | async-start | bytes 3276800 | tf_op jit(solution)/shard_map/reduce_scatter | solution.py:224
  574.1 139.4 %reduce-scatter.47.cloned.1.call-start = ((), (), s32[]{:S(2)}) async-start(), calls=%async_computation.49 | async-start | bytes 3276800 | tf_op jit(solution)/shard_map/reduce_scatter | solution.py:224
  613.6 128.8 %reduce-scatter.33.cloned.1.call-start = ((), (), s32[]{:S(2)}) async-start(), calls=%async_computation.37 | async-start | bytes 1638400 | tf_op jit(solution)/shard_map/reduce_scatter | solution.py:199
  619.9 151.9 %reduce-scatter.37.cloned.1.call-start = ((), (), s32[]{:S(2)}) async-start(), calls=%async_computation.43 | async-start | bytes 1638400 | tf_op jit(solution)/shard_map/reduce_scatter | solution.py:199
  626.1 174.6 %reduce-scatter.29.cloned.1.call-start = ((), (), s32[]{:S(2)}) async-start(), calls=%async_computation.31 | async-start | bytes 1638400 | tf_op jit(solution)/shard_map/reduce_scatter | solution.py:199
  632.2 173.4 %all-gather.54.cloned.1.call-start = ((), (), s32[]{:S(2)}) async-start(), calls=%async_computation.50 | async-start | bytes 1638400 | tf_op jit(solution)/shard_map/all_gather | solution.py:237
  745.6 105.8 %all-gather.52.cloned.1.call-start = ((), (), s32[]{:S(2)}) async-start(), calls=%async_computation.45 | async-start | bytes 1638400 | tf_op jit(solution)/shard_map/all_gather | solution.py:237
  804.9 92.1 %all-gather.56.cloned.1.call-start = ((), (), s32[]{:S(2)}) async-start(), calls=%async_computation.55 | async-start | bytes 1638400 | tf_op jit(solution)/shard_map/all_gather | solution.py:237
  805.5 150.3 %reduce-scatter.49.cloned.1.call-start = ((), (), s32[]{:S(2)}) async-start(), calls=%async_computation.51 | async-start | bytes 3276800 | tf_op jit(solution)/shard_map/reduce_scatter | solution.py:265
  839.7 118.2 %reduce-scatter.51.cloned.1.call-start = ((), (), s32[]{:S(2)}) async-start(), calls=%async_computation.52 | async-start | bytes 3276800 | tf_op jit(solution)/shard_map/reduce_scatter | solution.py:266
  850.7 155.1 %reduce-scatter.41.cloned.1.call-start = ((), (), s32[]{:S(2)}) async-start(), calls=%async_computation.46 | async-start | bytes 3276800 | tf_op jit(solution)/shard_map/reduce_scatter | solution.py:265
  885.2 174.8 %reduce-scatter.43.cloned.1.call-start = ((), (), s32[]{:S(2)}) async-start(), calls=%async_computation.47 | async-start | bytes 3276800 | tf_op jit(solution)/shard_map/reduce_scatter | solution.py:266
  896.3 217.6 %reduce-scatter.57.cloned.1.call-start = ((), (), s32[]{:S(2)}) async-start(), calls=%async_computation.56 | async-start | bytes 3276800 | tf_op jit(solution)/shard_map/reduce_scatter | solution.py:265
  931.0 237.1 %reduce-scatter.59.cloned.1.call-start = ((), (), s32[]{:S(2)}) async-start(), calls=%async_computation.57 | async-start | bytes 3276800 | tf_op jit(solution)/shard_map/reduce_scatter | solution.py:266
  942.1 284.2 %reduce-scatter.53.cloned.1.call-start = ((), (), s32[]{:S(2)}) async-start(), calls=%async_computation.53 | async-start | bytes 1638400 | tf_op jit(solution)/shard_map/reduce_scatter | solution.py:297
  963.9 262.4 %reduce-scatter.45.cloned.1.call-start = ((), (), s32[]{:S(2)}) async-start(), calls=%async_computation.48 | async-start | bytes 1638400 | tf_op jit(solution)/shard_map/reduce_scatter | solution.py:297
  1065.9 188.5 %reduce-scatter.61.cloned.1.call-start = ((), (), s32[]{:S(2)}) async-start(), calls=%async_computation.58 | async-start | bytes 1638400 | tf_op jit(solution)/shard_map/reduce_scatter | solution.py:297
  1174.1 152.0 %reduce-scatter.69.cloned.1.call-start = ((), (), s32[]{:S(2)}) async-start(), calls=%async_computation.65 | async-start | bytes 2211840 | tf_op jit(solution)/shard_map/reduce_scatter | solution.py:311
  1180.6 216.2 %reduce-scatter.63.cloned.1.call-start = ((), (), s32[]{:S(2)}) async-start(), calls=%async_computation.62 | async-start | bytes 2211840 | tf_op jit(solution)/shard_map/reduce_scatter | solution.py:308
  1186.2 335.4 %reduce-scatter.73.cloned.1.call-start = ((), (), s32[]{:S(2)}) async-start(), calls=%async_computation.67 | async-start | bytes 7372800
  1205.7 441.2 %reduce-scatter.71.cloned.1.call-start = ((), (), s32[]{:S(2)}) async-start(), calls=%async_computation.66 | async-start | bytes 7372800 | tf_op jit(solution)/shard_map/reduce_scatter | solution.py:312
  1216.8 430.0 %all-reduce.3.cloned.1.call-start = ((), (), s32[]{:S(2)}) async-start(), calls=%async_computation.68 | async-start | bytes 188416 | tf_op jit(solution)/shard_map/psum | solution.py:328
  1257.8 459.9 %reduce-scatter.67.cloned.1.call-start = ((), (), s32[]{:S(2)}) async-start(), calls=%async_computation.64 | async-start | bytes 2211840 | tf_op jit(solution)/shard_map/reduce_scatter | solution.py:310
  1262.0 526.1 %reduce-scatter.65.cloned.1.call-start = ((), (), s32[]{:S(2)}) async-start(), calls=%async_computation.63 | async-start | bytes 2211840 | tf_op jit(solution)/shard_map/reduce_scatter | solution.py:309
  (190 other events, 3103.3 us)
Sparse Core Ops, SparseCore 0:
  13.4 20.8 all-gather.23
  36.5 18.1 all-gather.43
  56.8 18.1 all-gather.35
  76.4 39.3 all-gather.27
  120.7 42.6 all-gather.25
  164.8 45.2 all-gather.47
  211.7 31.6 all-gather.45
  244.9 31.6 all-gather.39
  278.2 31.6 all-gather.37
  312.2 33.6 reduce-scatter.26
  348.4 34.4 reduce-scatter.34
  385.3 34.4 reduce-scatter.30
  745.7 18.1 all-gather.53
  805.0 18.1 all-gather.51
  825.2 18.1 all-gather.55
  845.6 52.2 reduce-scatter.48
  900.0 51.7 reduce-scatter.50
  954.0 51.7 reduce-scatter.40
  1008.2 51.7 reduce-scatter.42
  1062.1 51.7 reduce-scatter.56
  1116.3 51.7 reduce-scatter.58
  1170.7 25.9 reduce-scatter.52
  1199.2 26.3 reduce-scatter.44
  1228.0 26.4 reduce-scatter.60
  1258.5 67.5 reduce-scatter.68
  1329.9 66.8 reduce-scatter.62
  1400.9 120.6 reduce-scatter.72
  1525.8 120.9 reduce-scatter.70
  1650.9 66.7 reduce-scatter.66
  1721.6 66.4 reduce-scatter.64
Sparse Core Ops, SparseCore 1:
  322.7 60.4 all-gather.31
  423.8 18.0 all-gather.29
  443.3 18.0 all-gather.57
  463.5 61.3 all-gather.33
  526.9 16.7 all-gather.49
  545.2 18.0 all-gather.61
  565.3 18.0 all-gather.41
  584.8 18.0 all-gather.59
  605.3 34.3 reduce-scatter.38
  642.2 34.4 reduce-scatter.54
  679.0 34.4 reduce-scatter.46
  716.0 26.3 reduce-scatter.32
  745.4 26.3 reduce-scatter.36
  774.3 26.3 reduce-scatter.28
  1257.9 138.5 all-reduce.2
